TPU v7x, 512 devices: a whole 4x8x8 slice. The times are simulated.
512 devices in a mesh: wide: 128 (over y, z, core), rep: 4 (over x).
Axes of the slice: x: 4, y: 8, z: 8, core: 2. Of those that a mesh axis runs over, the one named last changes fastest.
Arguments:
- node_feats: bfloat16 [131072, 512], P('wide'), may hold values from -6 to 6
- w_self: bfloat16 [512, 512], replicated, may hold values from -0.25 to 0.25
- w_neigh: bfloat16 [512, 512], replicated, may hold values from -0.25 to 0.25
- send_rows: int32 [128, 128, 32], P('wide', None, 'rep'), may hold values from 0 to 1023
- tile_dst: int32 [128, 4, 128], P('wide', 'rep'), may hold values from 0 to 15
- tile_src: int32 [128, 4, 128], P('wide', 'rep'), may hold values from 0 to 31
- tile_bits: int32 [128, 4, 32768], P('wide', 'rep'), may hold values from 0 to 65280
- norm_count: int32 [131072], P('wide'), may hold values from 512 to 2048
- grad_out: bfloat16 [131072, 512], P(('wide', 'rep')), may hold values from -6 to 6
Outputs:
- out_feats: bfloat16 [131072, 512], P(('wide', 'rep'))
- grad_feats: bfloat16 [131072, 512], P(('wide', 'rep'))
- grad_self: bfloat16 [512, 512], replicated
- grad_neigh: bfloat16 [512, 512], replicated
All inputs are finite; a program needn't handle non-finite values.
Results may differ from a plain program's by a relative error of at most 0.014.
Values may be sent and summed in bfloat16 or wider, within the bound.
No kernel may reach another device: no remote copies, remote signals or barrier semaphores. Data moves between devices by JAX's collectives and lax.ppermute only.
A program may use at most 64 MiB of HBM per device.

v0:
```python
import math
import jax
import jax.numpy as jnp
from jax import lax
from jax.sharding import PartitionSpec as P

BLOCK = 64


def unpack_bits(packed, tile_count, block_size):
    shaped = packed.reshape(tile_count, block_size, block_size // 16)
    shift_list = jnp.arange(16, dtype=jnp.int32)
    bit_grid = jnp.bitwise_and(jnp.right_shift(shaped[..., None], shift_list), 1)
    return bit_grid.reshape(tile_count, block_size, block_size)


def times_transposed(left, right):
    return lax.dot_general(
        left, right, (((1,), (1,)), ((), ())), preferred_element_type=jnp.float32
    )


def on_device(
    node_feats, w_self, w_neigh, send_rows, tile_dst, tile_src, tile_bits, norm_count, grad_out
):
    node_rows, feat_width = node_feats.shape
    peer_count = lax.axis_size("wide")
    replicas = lax.axis_size("rep")
    slot_count = send_rows.shape[2]
    tile_total = tile_dst.shape[2]
    block_size = BLOCK
    quarter = node_rows // replicas
    rep_index = lax.axis_index("rep")
    dst_count = node_rows // block_size
    group_size = math.gcd(tile_total, 32)
    send_index = send_rows[0]
    outgoing = jnp.take(node_feats, send_index.reshape(-1), axis=0).reshape(
        peer_count, slot_count, feat_width
    )
    incoming = lax.all_to_all(outgoing, "wide", split_axis=0, concat_axis=0, tiled=True)
    src_table = jnp.concatenate(
        [node_feats, incoming.reshape(peer_count * slot_count, feat_width)], axis=0
    )
    source_blocks = src_table.reshape(-1, block_size, feat_width)
    src_count = source_blocks.shape[0]
    tile_masks = unpack_bits(tile_bits[0, 0], tile_total, block_size).astype(jnp.bfloat16)
    grouped_masks = tile_masks.reshape(-1, group_size, block_size, block_size)
    grouped_dst = tile_dst[0, 0].reshape(-1, group_size)
    grouped_src = tile_src[0, 0].reshape(-1, group_size)

    def forward_group(running, group_items):
        mask_part, dst_part, src_part = group_items
        picked = jnp.take(source_blocks, src_part, axis=0)
        products = jnp.einsum("tij,tjf->tif", mask_part, picked, preferred_element_type=jnp.float32)
        return (running.at[dst_part].add(products), None)

    partial_sum, _ = lax.scan(
        forward_group,
        jnp.zeros((dst_count, block_size, feat_width), jnp.float32),
        (grouped_masks, grouped_dst, grouped_src),
    )
    partial_sum = partial_sum.reshape(node_rows, feat_width)
    summed = lax.psum(partial_sum, "rep")
    own_sums = lax.dynamic_slice_in_dim(summed, rep_index * quarter, quarter, 0)
    scale_all = lax.rsqrt(norm_count.astype(jnp.float32))
    own_scale = lax.dynamic_slice_in_dim(scale_all, rep_index * quarter, quarter, 0)
    own_feats = lax.dynamic_slice_in_dim(node_feats, rep_index * quarter, quarter, 0)
    own_agg = (own_sums * own_scale[:, None]).astype(jnp.bfloat16)
    pre_act = jnp.dot(own_feats, w_self, preferred_element_type=jnp.float32) + jnp.dot(
        own_agg, w_neigh, preferred_element_type=jnp.float32
    )
    sigmoid = jax.nn.sigmoid(pre_act)
    out_feats = (pre_act * sigmoid).astype(jnp.bfloat16)
    grad_pre = (grad_out.astype(jnp.float32) * sigmoid * (1.0 + pre_act * (1.0 - sigmoid))).astype(
        jnp.bfloat16
    )
    dims_rows = (((0,), (0,)), ((), ()))
    self_term = lax.dot_general(own_feats, grad_pre, dims_rows, preferred_element_type=jnp.float32)
    neigh_term = lax.dot_general(own_agg, grad_pre, dims_rows, preferred_element_type=jnp.float32)
    summed_self, summed_neigh = lax.psum((self_term, neigh_term), ("wide", "rep"))
    own_grad_agg = (times_transposed(grad_pre, w_neigh) * own_scale[:, None]).astype(jnp.bfloat16)
    grad_agg = lax.all_gather(own_grad_agg, "rep", axis=0, tiled=True)
    agg_blocks = grad_agg.reshape(dst_count, block_size, feat_width)

    def backward_group(running, group_items):
        mask_part, dst_part, src_part = group_items
        picked = jnp.take(agg_blocks, dst_part, axis=0)
        products = jnp.einsum("tij,tif->tjf", mask_part, picked, preferred_element_type=jnp.float32)
        return (running.at[src_part].add(products), None)

    table_grad, _ = lax.scan(
        backward_group,
        jnp.zeros((src_count, block_size, feat_width), jnp.float32),
        (grouped_masks, grouped_dst, grouped_src),
    )
    table_grad = table_grad.reshape(src_count * block_size, feat_width)
    local_grad = table_grad[:node_rows]
    halo_grad = (
        table_grad[node_rows:].astype(jnp.bfloat16).reshape(peer_count, slot_count, feat_width)
    )
    returned = lax.all_to_all(halo_grad, "wide", split_axis=0, concat_axis=0, tiled=True)
    returned_rows = (
        jnp.zeros((node_rows, feat_width), jnp.float32)
        .at[send_index.reshape(-1)]
        .add(returned.reshape(-1, feat_width).astype(jnp.float32))
    )
    own_total = lax.psum_scatter(
        (local_grad + returned_rows).astype(jnp.bfloat16), "rep", scatter_dimension=0, tiled=True
    ).astype(jnp.float32)
    grad_feats = (own_total + times_transposed(grad_pre, w_self)).astype(jnp.bfloat16)
    return (
        out_feats,
        grad_feats,
        summed_self.astype(jnp.bfloat16),
        summed_neigh.astype(jnp.bfloat16),
    )


def solution(mesh):
    in_specs = (
        P("wide", None),
        P(),
        P(),
        P("wide", None, "rep"),
        P("wide", "rep", None),
        P("wide", "rep", None),
        P("wide", "rep", None),
        P("wide"),
        P(("wide", "rep"), None),
    )
    out_specs = (P(("wide", "rep"), None), P(("wide", "rep"), None), P(), P())
    return jax.shard_map(
        on_device, mesh=mesh, in_specs=in_specs, out_specs=out_specs, check_vma=False
    )
```

profile of v0, /device:TPU:1, one launch (start us, length us, event | category | flops | bytes accessed | tf_op | source)
XLA Modules:
  0.0 459.9 jit_solution(16109861953868291241)
XLA Ops:
  7.2 0.8 compare_and_fusion.2
  7.9 0.8 copy.18
  8.7 0.1 copy.17
  8.8 0.1 reshape_squeeze.15
  9.0 5.4 %gather_fusion.2 = bf16[1024,512]{1,0:T(8,128)(2,1)S(1)} fusion(bf16[1024,512]{1,0:T(8,128)(2,1)} %param.13, s32[1024]{0:T(1024)S(1)} %broadcast_clamp_fusion), kind=kCustom, calls=%fused_computation.2 | custom fusion | bytes 2101248 | tf_op jit(solution)/shard_map/jit(_take)/gather | solution.py:37
  14.4 1.2 bitcast_select_fusion
  15.5 18.4 %all-to-all-start = ((bf16[128,8,512]{2,1,0:T(8,128)(2,1)}), bf16[128,8,512]{2,1,0:T(8,128)(2,1)S(1)}, u32[]{:S(2)}, u32[]{:S(2)}) async-start(bf16[128,8,512]{2,1,0:T(8,128)(2,1)} %bitcast_select_fusion), calls=%async_computation | async-start | bytes 2097152 | tf_op jit(solution)/shard_map/all_to_all | solution.py:40
  34.0 0.5 broadcast.165
  34.5 0.7 reduce.9
  35.2 0.7 reduce.11
  35.9 0.1 reshape_squeeze.13
  36.0 0.1 shift_right_arithmetic.27
  36.1 1.0 reduce.10
  37.1 5.7 %shift_right_arithmetic.23 = s32[128,64,4]{2,1,0:T(8,128)} reshape(s32[32768]{0:T(1024)S(1)} %reduce.10) | data formatting | bytes 262144 | tf_op jit(solution)/shard_map/shift_right_arithmetic | solution.py:13
  42.7 3.0 copy.16
  45.7 0.3 shift_right_arithmetic.24
  46.1 2.1 and_convert_fusion
  48.2 16.2 %all-to-all-done = bf16[128,8,512]{2,1,0:T(8,128)(2,1)S(1)} async-done(((bf16[128,8,512]{2,1,0:T(8,128)(2,1)}), bf16[128,8,512]{2,1,0:T(8,128)(2,1)S(1)}, u32[]{:S(2)}, u32[]{:S(2)}) %all-to-all-start) | async-done | bytes 1048608 | tf_op jit(solution)/shard_map/all_to_all | solution.py:40
  64.4 1.5 pad_maximum_fusion
  65.9 0.2 broadcast_in_dim.43
  66.1 58.5 %while.20 = (s32[]{:T(128)}, f32[16,64,512]{2,1,0:T(8,128)S(1)}, s32[4,32]{1,0:T(4,128)S(1)}, bf16[4,32,64,64]{2,3,1,0:T(8,128)(2,1)}, s32[4,32]{1,0:T(4,128)S(1)}, /*index=5*/bf16[32,64,512]{2,1,0:T(8,128)(2,1)}, s32[]{:T(128)}) while((s32[]{:T(128)}, f32[16,64,512]{2,1,0:T(8,128)S(1)}, s32[4,32]{1,0:T(4,128)S(1)}, ...), condition=%wide.region_2.3_spmd, body=%wide.region_0.0_spmd.sunk | while | flops 136316288 | bytes 23598240 | solution.py:57
  66.2 3.6 gather_fusion
  69.8 4.5 fusion.53
  74.3 6.5 %scatter_fusion = f32[16,64,512]{2,1,0:T(8,128)S(1)} fusion(f32[16,64,512]{2,1,0:T(8,128)S(1)} %get-tuple-element.204, s32[32]{0:T(128)S(1)} %get-tuple-element.186, f32[32,64,512]{2,1,0:T(8,128)} %fusion.53), kind=kCustom, calls=%fused_computation.3.clone.1 | custom fusion | flops 1048576 | bytes 12583040 | tf_op jit(solution)/shard_map/while/body/eval_jaxpr/scatter-add | solution.py:55
  80.8 3.6 gather_fusion
  84.4 4.5 fusion.53
  88.9 6.5 %scatter_fusion = f32[16,64,512]{2,1,0:T(8,128)S(1)} fusion(f32[16,64,512]{2,1,0:T(8,128)S(1)} %get-tuple-element.204, s32[32]{0:T(128)S(1)} %get-tuple-element.186, f32[32,64,512]{2,1,0:T(8,128)} %fusion.53), kind=kCustom, calls=%fused_computation.3.clone.1 | custom fusion | flops 1048576 | bytes 12583040 | tf_op jit(solution)/shard_map/while/body/eval_jaxpr/scatter-add | solution.py:55
  95.4 3.6 gather_fusion
  99.1 4.5 fusion.53
  103.5 6.5 %scatter_fusion = f32[16,64,512]{2,1,0:T(8,128)S(1)} fusion(f32[16,64,512]{2,1,0:T(8,128)S(1)} %get-tuple-element.204, s32[32]{0:T(128)S(1)} %get-tuple-element.186, f32[32,64,512]{2,1,0:T(8,128)} %fusion.53), kind=kCustom, calls=%fused_computation.3.clone.1 | custom fusion | flops 1048576 | bytes 12583040 | tf_op jit(solution)/shard_map/while/body/eval_jaxpr/scatter-add | solution.py:55
  110.1 3.6 gather_fusion
  113.7 4.5 fusion.53
  118.2 6.5 %scatter_fusion = f32[16,64,512]{2,1,0:T(8,128)S(1)} fusion(f32[16,64,512]{2,1,0:T(8,128)S(1)} %get-tuple-element.204, s32[32]{0:T(128)S(1)} %get-tuple-element.186, f32[32,64,512]{2,1,0:T(8,128)} %fusion.53), kind=kCustom, calls=%fused_computation.3.clone.1 | custom fusion | flops 1048576 | bytes 12583040 | tf_op jit(solution)/shard_map/while/body/eval_jaxpr/scatter-add | solution.py:55
  124.7 1.3 copy-done.1
  126.0 0.2 all-gather.2.cloned.1.call-start
  126.4 1.2 fusion.29
  127.6 62.0 %all-reduce.4.cloned.1.call-done = f32[1024,512]{1,0:T(8,128)} async-done(((f32[1024,512]{1,0:T(8,128)}), f32[1024,512]{1,0:T(8,128)}) %all-reduce.4.cloned.1.call-update) | async-done | bytes 2097168 | tf_op jit(solution)/shard_map/psum | solution.py:63
  189.6 2.3 multiply_convert_fusion
  192.0 1.0 fusion.24
  193.0 28.4 %all-gather.2.cloned.1.call-done = bf16[1024,512]{1,0:T(8,128)(2,1)} async-done(((bf16[256,512]{1,0:T(8,128)(2,1)}), bf16[1024,512]{1,0:T(8,128)(2,1)}) %all-gather.2.cloned.1.call-update) | async-done | bytes 1048592 | tf_op jit(solution)/shard_map/all_gather | solution.py:82
  221.4 2.5 broadcast_in_dim.46
  223.9 62.5 %while.21 = (s32[]{:T(128)}, f32[32,64,512]{2,1,0:T(8,128)}, s32[4,32]{1,0:T(4,128)S(1)}, bf16[4,32,64,64]{2,3,1,0:T(8,128)(2,1)}, s32[4,32]{1,0:T(4,128)S(1)}, /*index=5*/bf16[16,64,512]{2,1,0:T(8,128)(2,1)}, s32[]{:T(128)}) while((s32[]{:T(128)}, f32[32,64,512]{2,1,0:T(8,128)}, s32[4,32]{1,0:T(4,128)S(1)}, ...), condition=%wide.region_6.7_spmd, body=%wide.region_4.6_spmd.sunk | while | flops 136316288 | bytes 23598240 | solution.py:91
  224.0 1.9 gather_fusion.1
  225.9 3.8 fusion.57
  229.7 9.8 %scatter_fusion.1 = f32[32,64,512]{2,1,0:T(8,128)} fusion(f32[32,64,512]{2,1,0:T(8,128)} %get-tuple-element.225, s32[32]{0:T(128)S(1)} %get-tuple-element.194, f32[32,64,512]{2,1,0:T(8,128)} %fusion.57), kind=kCustom, calls=%fused_computation.4.clone.1 | custom fusion | flops 1048576 | bytes 12583040 | tf_op jit(solution)/shard_map/while/body/eval_jaxpr/scatter-add | solution.py:89
  239.5 1.9 gather_fusion.1
  241.4 3.7 fusion.57
  245.1 9.8 %scatter_fusion.1 = f32[32,64,512]{2,1,0:T(8,128)} fusion(f32[32,64,512]{2,1,0:T(8,128)} %get-tuple-element.225, s32[32]{0:T(128)S(1)} %get-tuple-element.194, f32[32,64,512]{2,1,0:T(8,128)} %fusion.57), kind=kCustom, calls=%fused_computation.4.clone.1 | custom fusion | flops 1048576 | bytes 12583040 | tf_op jit(solution)/shard_map/while/body/eval_jaxpr/scatter-add | solution.py:89
  255.0 1.9 gather_fusion.1
  256.9 3.7 fusion.57
  260.6 10.0 %scatter_fusion.1 = f32[32,64,512]{2,1,0:T(8,128)} fusion(f32[32,64,512]{2,1,0:T(8,128)} %get-tuple-element.225, s32[32]{0:T(128)S(1)} %get-tuple-element.194, f32[32,64,512]{2,1,0:T(8,128)} %fusion.57), kind=kCustom, calls=%fused_computation.4.clone.1 | custom fusion | flops 1048576 | bytes 12583040 | tf_op jit(solution)/shard_map/while/body/eval_jaxpr/scatter-add | solution.py:89
  270.7 1.9 gather_fusion.1
  272.6 3.7 fusion.57
  276.3 10.1 %scatter_fusion.1 = f32[32,64,512]{2,1,0:T(8,128)} fusion(f32[32,64,512]{2,1,0:T(8,128)} %get-tuple-element.225, s32[32]{0:T(128)S(1)} %get-tuple-element.194, f32[32,64,512]{2,1,0:T(8,128)} %fusion.57), kind=kCustom, calls=%fused_computation.4.clone.1 | custom fusion | flops 1048576 | bytes 12583040 | tf_op jit(solution)/shard_map/while/body/eval_jaxpr/scatter-add | solution.py:89
  286.4 2.8 slice.22
  289.2 15.9 %all-to-all-start.1 = ((bf16[128,8,512]{2,1,0:T(8,128)(2,1)}), bf16[128,8,512]{2,1,0:T(8,128)(2,1)}, u32[]{:S(2)}, u32[]{:S(2)}) async-start(bf16[128,8,512]{2,1,0:T(8,128)(2,1)} %bitcast.21), calls=%async_computation.1 | async-start | bytes 2097152 | tf_op jit(solution)/shard_map/all_to_all | solution.py:101
  305.1 1.9 slice.11
  307.0 28.2 %all-to-all-done.1 = bf16[128,8,512]{2,1,0:T(8,128)(2,1)} async-done(((bf16[128,8,512]{2,1,0:T(8,128)(2,1)}), bf16[128,8,512]{2,1,0:T(8,128)(2,1)}, u32[]{:S(2)}, u32[]{:S(2)}) %all-to-all-start.1) | async-done | bytes 1048608 | tf_op jit(solution)/shard_map/all_to_all | solution.py:101
  335.2 8.0 %scatter_custom_fusion.2 = f32[1024,512]{1,0:T(8,128)S(1)} fusion(f32[1024,512]{1,0:T(8,128)S(1)} %bitcast.83, s32[1024]{0:T(1024)S(1)} %bitcast.86, bf16[128,8,512]{2,1,0:T(8,128)(2,1)} %all-to-all-done.1), kind=kCustom, calls=%fused_computation.45 | custom fusion | flops 1048576 | bytes 3145728 | tf_op jit(solution)/shard_map/scatter-add | solution.py:105
  343.2 1.1 convert_element_type.58
  344.3 1.5 fusion.33
  345.8 1.3 fusion.27
  347.0 104.4 %all-reduce.5 = (bf16[512,512]{1,0:T(8,128)(2,1)}, bf16[512,512]{1,0:T(8,128)(2,1)}) all-reduce(f32[512,512]{1,0:T(8,128)S(1)} %fusion.27, f32[512,512]{1,0:T(8,128)S(1)} %fusion.33), channel_id=1, replica_groups=mesh['wide'=128,'rep'=4] {'wide','rep'}, use_global_device_ids=true, to_apply=%region_9.10 | all-reduce | flops 524288 | bytes 3145728 | tf_op jit(solution)/shard_map/psum | solution.py:80
  451.4 2.0 fusion.25
  (51 shorter events, 0.6 us)
Async XLA Ops:
  7.2 182.5 %copy-start = (bf16[512,512]{1,0:T(8,128)(2,1)S(1)}, bf16[512,512]{1,0:T(8,128)(2,1)}, u32[]{:S(2)}) copy-start(bf16[512,512]{1,0:T(8,128)(2,1)} %param.15) | copy-start | bytes 1572868
  14.3 20.2 %copy-start.6 = (s32[1,1,128]{2,1,0:T(1,128)S(1)}, s32[1,1,128]{2,1,0:T(1,128)}, u32[]{:S(2)}) copy-start(s32[1,1,128]{2,1,0:T(1,128)} %param.17) | copy-start | bytes 1540
  14.3 20.9 %copy-start.7 = (s32[1,1,128]{2,1,0:T(1,128)S(1)}, s32[1,1,128]{2,1,0:T(1,128)}, u32[]{:S(2)}) copy-start(s32[1,1,128]{2,1,0:T(1,128)} %param.18) | copy-start | bytes 1540
  14.4 21.8 %copy-start.4 = (s32[1,1,32768]{2,1,0:T(1,128)S(1)}, s32[1,1,32768]{2,1,0:T(1,128)}, u32[]{:S(2)}) copy-start(s32[1,1,32768]{2,1,0:T(1,128)} %param.19) | copy-start | bytes 393220
  15.5 48.9 %all-to-all-start = ((bf16[128,8,512]{2,1,0:T(8,128)(2,1)}), bf16[128,8,512]{2,1,0:T(8,128)(2,1)S(1)}, u32[]{:S(2)}, u32[]{:S(2)}) async-start(bf16[128,8,512]{2,1,0:T(8,128)(2,1)} %bitcast_select_fusion), calls=%async_computation | async-start | bytes 2097152 | tf_op jit(solution)/shard_map/all_to_all | solution.py:40
  34.0 155.7 %all-reduce.4.cloned.1.call-start = ((), (), s32[]{:S(2)}) async-start(), calls=%async_computation.3 | async-start | bytes 4194304 | tf_op jit(solution)/shard_map/psum | solution.py:63
  46.1 18.3 %copy-start.2 = (bf16[1024,512]{1,0:T(8,128)(2,1)S(1)}, bf16[1024,512]{1,0:T(8,128)(2,1)}, u32[]{:S(2)}) copy-start(bf16[1024,512]{1,0:T(8,128)(2,1)} %param.13) | copy-start | bytes 3145732
  124.7 1.3 copy-start.1
  124.7 1.6 copy-start.5
  124.7 1.7 copy-start.3
  126.0 95.4 %all-gather.2.cloned.1.call-start = ((), (), s32[]{:S(2)}) async-start(), calls=%async_computation.4 | async-start | bytes 1310720 | tf_op jit(solution)/shard_map/all_gather | solution.py:82
  289.2 46.0 %all-to-all-start.1 = ((bf16[128,8,512]{2,1,0:T(8,128)(2,1)}), bf16[128,8,512]{2,1,0:T(8,128)(2,1)}, u32[]{:S(2)}, u32[]{:S(2)}) async-start(bf16[128,8,512]{2,1,0:T(8,128)(2,1)} %bitcast.21), calls=%async_computation.1 | async-start | bytes 2097152 | tf_op jit(solution)/shard_map/all_to_all | solution.py:101
  305.1 146.3 %reduce-scatter.2.cloned.1.call-start = ((), (), s32[]{:S(2)}) async-start(), calls=%async_computation.5 | async-start | bytes 1310720 | tf_op jit(solution)/shard_map/reduce_scatter | solution.py:107
Sparse Core Ops, SparseCore 0:
  126.2 63.4 all-reduce.3
  193.2 28.2 all-gather.1
  344.4 20.2 reduce-scatter.1
where the time goes:
time: 462 us; the launch traced here: 460 us
  waiting for transfers between devices  135 us (29%)
  blocking collectives  104 us (23%)
  other arithmetic  82.7 us (18%)
  local copies, waits for them, and re-layouts  47 us (10%)
  matrix products  42.2 us (9%)
  starting transfers between devices  34.6 us (7%)
  between operations  14 us (3%)
    psum x1, blocking collectives, on_device(): lax.psum((self_term, neigh_term), ('wide', 'rep'))  104 us
    psum x1, waiting for transfers between devices, on_device(): summed = lax.psum(partial_sum, 'rep')  62 us
    scatter-add x4, other arithmetic, backward_group(): return (running.at[src_part].add(products), None)  39.6 us
    all_gather x1, waiting for transfers between devices, on_device(): grad_agg = lax.all_gather(own_grad_agg, 'rep', axis=0, tiled=True)  28.4 us
    all_to_all x1, waiting for transfers between devices, on_device(): lax.all_to_all(halo_grad, 'wide', split_axis=0, concat_axis=0, tiled=True)  28.2 us
    scatter-add x4, other arithmetic, forward_group(): return (running.at[dst_part].add(products), None)  25.9 us
    all_to_all x1, starting transfers between devices, on_device(): lax.all_to_all(outgoing, 'wide', split_axis=0, concat_axis=0, tiled=True)  18.4 us
    dot_general x4, matrix products, forward_group(): jnp.einsum('tij,tjf->tif', mask_part, picked, preferred_element_type=jnp....  17.9 us
  transfers between devices with their start and end apart: 5, of which 4 were waited for; matrix products, arithmetic and copies ran while one was open for 4% of the time, Pallas kernels for 0%

commit v1 on v0

--- a/solution.py
+++ b/solution.py
@@ -5,6 +5,14 @@
 from jax.sharding import PartitionSpec as P
 
 BLOCK = 64
+
+
+def doubling_sum(x, axis):
+    devices, result = (lax.axis_size(axis), x)
+    for far in [1 << k for k in range(devices.bit_length() - 1)]:
+        swap = [(i, i ^ far) for i in range(devices)]
+        result = result + lax.ppermute(result, axis, swap)
+    return result
 
 
 def unpack_bits(packed, tile_count, block_size):
@@ -60,7 +68,7 @@
         (grouped_masks, grouped_dst, grouped_src),
     )
     partial_sum = partial_sum.reshape(node_rows, feat_width)
-    summed = lax.psum(partial_sum, "rep")
+    summed = doubling_sum(partial_sum, "rep")
     own_sums = lax.dynamic_slice_in_dim(summed, rep_index * quarter, quarter, 0)
     scale_all = lax.rsqrt(norm_count.astype(jnp.float32))
     own_scale = lax.dynamic_slice_in_dim(scale_all, rep_index * quarter, quarter, 0)

time: 462 us -> 495 us (1.071)
  waiting for transfers between devices: 135 us -> 158 us
  starting transfers between devices: 34.6 us -> 42.3 us
    ppermute x0 -> x2, waiting for transfers between devices: none -> 86.9 us  [doubling_sum(): result = result + lax.ppermute(result, axis, swap)]
    psum x1 -> x0, waiting for transfers between devices: 62 us -> none  [on_device(): summed = lax.psum(partial_sum, 'rep')]
    ppermute x0 -> x2, starting transfers between devices: none -> 8 us  [doubling_sum(): result = result + lax.ppermute(result, axis, swap)]
  transfers between devices with their start and end apart: 5 -> 6, of which waited for: 4 -> 5; matrix products, arithmetic and copies ran while one was open for 4% -> 4% of each run, Pallas kernels for 0% -> 0%
where the time goes in v1:
time: 495 us; the launch traced here: 493 us
  waiting for transfers between devices  158 us (32%)
  blocking collectives  105 us (21%)
  other arithmetic  85.6 us (17%)
  local copies, waits for them, and re-layouts  46.4 us (9%)
  starting transfers between devices  42.3 us (9%)
  matrix products  41.8 us (8%)
  between operations  14.3 us (3%)
    psum x1, blocking collectives, on_device(): lax.psum((self_term, neigh_term), ('wide', 'rep'))  105 us
    ppermute x2, waiting for transfers between devices, doubling_sum(): result = result + lax.ppermute(result, axis, swap)  86.9 us
    scatter-add x4, other arithmetic, backward_group(): return (running.at[src_part].add(products), None)  39.6 us
    all_to_all x1, waiting for transfers between devices, on_device(): lax.all_to_all(halo_grad, 'wide', split_axis=0, concat_axis=0, tiled=True)  28.2 us
    all_gather x1, waiting for transfers between devices, on_device(): grad_agg = lax.all_gather(own_grad_agg, 'rep', axis=0, tiled=True)  26.6 us
    scatter-add x4, other arithmetic, forward_group(): return (running.at[dst_part].add(products), None)  25.9 us
    all_to_all x1, starting transfers between devices, on_device(): lax.all_to_all(outgoing, 'wide', split_axis=0, concat_axis=0, tiled=True)  18.4 us
    dot_general x4, matrix products, forward_group(): jnp.einsum('tij,tjf->tif', mask_part, picked, preferred_element_type=jnp....  17.9 us
  transfers between devices with their start and end apart: 6, of which 5 were waited for; matrix products, arithmetic and copies ran while one was open for 4% of the time, Pallas kernels for 0%

profile of v1, /device:TPU:1, one launch (start us, length us, event | category | flops | bytes accessed | tf_op | source)
XLA Modules:
  0.0 493.0 jit_solution(9854447556488763968)
XLA Ops:
  7.2 0.8 copy.18
  8.0 0.7 compare_and_fusion.2
  9.0 5.3 %gather_fusion.2 = bf16[1024,512]{1,0:T(8,128)(2,1)S(1)} fusion(bf16[1024,512]{1,0:T(8,128)(2,1)} %param.13, s32[1024]{0:T(1024)S(1)} %broadcast_clamp_fusion), kind=kCustom, calls=%fused_computation.2 | custom fusion | bytes 2101248 | tf_op jit(solution)/shard_map/jit(_take)/gather | solution.py:45
  14.4 1.2 bitcast_select_fusion
  15.5 18.4 %all-to-all-start = ((bf16[128,8,512]{2,1,0:T(8,128)(2,1)}), bf16[128,8,512]{2,1,0:T(8,128)(2,1)S(1)}, u32[]{:S(2)}, u32[]{:S(2)}) async-start(bf16[128,8,512]{2,1,0:T(8,128)(2,1)} %bitcast_select_fusion), calls=%async_computation | async-start | bytes 2097152 | tf_op jit(solution)/shard_map/all_to_all | solution.py:48
  34.0 0.5 broadcast.165
  34.5 0.7 reduce.9
  35.3 1.0 reduce.10
  36.2 5.7 %shift_right_arithmetic.23 = s32[128,64,4]{2,1,0:T(8,128)} reshape(s32[32768]{0:T(1024)S(1)} %reduce.10) | data formatting | bytes 262144 | tf_op jit(solution)/shard_map/shift_right_arithmetic | solution.py:21
  41.9 3.0 copy.16
  45.0 0.7 reduce.11
  45.8 0.3 shift_right_arithmetic.24
  46.1 2.1 and_convert_fusion
  48.3 16.2 %all-to-all-done = bf16[128,8,512]{2,1,0:T(8,128)(2,1)S(1)} async-done(((bf16[128,8,512]{2,1,0:T(8,128)(2,1)}), bf16[128,8,512]{2,1,0:T(8,128)(2,1)S(1)}, u32[]{:S(2)}, u32[]{:S(2)}) %all-to-all-start) | async-done | bytes 1048608 | tf_op jit(solution)/shard_map/all_to_all | solution.py:48
  64.4 1.5 pad_maximum_fusion
  65.9 0.2 broadcast_in_dim.43
  66.1 58.5 %while.20 = (s32[]{:T(128)}, f32[16,64,512]{2,1,0:T(8,128)S(1)}, s32[4,32]{1,0:T(4,128)S(1)}, bf16[4,32,64,64]{2,3,1,0:T(8,128)(2,1)}, s32[4,32]{1,0:T(4,128)S(1)}, /*index=5*/bf16[32,64,512]{2,1,0:T(8,128)(2,1)}, s32[]{:T(128)}) while((s32[]{:T(128)}, f32[16,64,512]{2,1,0:T(8,128)S(1)}, s32[4,32]{1,0:T(4,128)S(1)}, ...), condition=%wide.region_2.3_spmd, body=%wide.region_0.0_spmd.sunk | while | flops 136316288 | bytes 23598240 | solution.py:65
  66.2 3.6 gather_fusion
  69.8 4.5 fusion.57
  74.3 6.5 %scatter_fusion = f32[16,64,512]{2,1,0:T(8,128)S(1)} fusion(f32[16,64,512]{2,1,0:T(8,128)S(1)} %get-tuple-element.204, s32[32]{0:T(128)S(1)} %get-tuple-element.186, f32[32,64,512]{2,1,0:T(8,128)} %fusion.57), kind=kCustom, calls=%fused_computation.3.clone.1 | custom fusion | flops 1048576 | bytes 12583040 | tf_op jit(solution)/shard_map/while/body/eval_jaxpr/scatter-add | solution.py:63
  80.8 3.6 gather_fusion
  84.4 4.5 fusion.57
  88.9 6.5 %scatter_fusion = f32[16,64,512]{2,1,0:T(8,128)S(1)} fusion(f32[16,64,512]{2,1,0:T(8,128)S(1)} %get-tuple-element.204, s32[32]{0:T(128)S(1)} %get-tuple-element.186, f32[32,64,512]{2,1,0:T(8,128)} %fusion.57), kind=kCustom, calls=%fused_computation.3.clone.1 | custom fusion | flops 1048576 | bytes 12583040 | tf_op jit(solution)/shard_map/while/body/eval_jaxpr/scatter-add | solution.py:63
  95.4 3.6 gather_fusion
  99.0 4.5 fusion.57
  103.5 6.5 %scatter_fusion = f32[16,64,512]{2,1,0:T(8,128)S(1)} fusion(f32[16,64,512]{2,1,0:T(8,128)S(1)} %get-tuple-element.204, s32[32]{0:T(128)S(1)} %get-tuple-element.186, f32[32,64,512]{2,1,0:T(8,128)} %fusion.57), kind=kCustom, calls=%fused_computation.3.clone.1 | custom fusion | flops 1048576 | bytes 12583040 | tf_op jit(solution)/shard_map/while/body/eval_jaxpr/scatter-add | solution.py:63
  110.1 3.6 gather_fusion
  113.7 4.5 fusion.57
  118.2 6.5 %scatter_fusion = f32[16,64,512]{2,1,0:T(8,128)S(1)} fusion(f32[16,64,512]{2,1,0:T(8,128)S(1)} %get-tuple-element.204, s32[32]{0:T(128)S(1)} %get-tuple-element.186, f32[32,64,512]{2,1,0:T(8,128)} %fusion.57), kind=kCustom, calls=%fused_computation.3.clone.1 | custom fusion | flops 1048576 | bytes 12583040 | tf_op jit(solution)/shard_map/while/body/eval_jaxpr/scatter-add | solution.py:63
  124.7 3.2 collective-permute-start
  127.9 44.6 %collective-permute-done = f32[1024,512]{1,0:T(8,128)S(1)} collective-permute-done((f32[1024,512]{1,0:T(8,128)S(1)}, f32[1024,512]{1,0:T(8,128)S(1)}, u32[]{:S(2)}, u32[]{:S(2)}) %collective-permute-start) | collective-permute-done | bytes 2097184 | tf_op jit(solution)/shard_map/ppermute | solution.py:14
  172.5 1.8 bitcast_add_fusion
  174.3 4.8 collective-permute-start.1
  179.2 1.2 fusion.31
  180.5 42.3 %collective-permute-done.1 = f32[1024,512]{1,0:T(8,128)S(1)} collective-permute-done((f32[1024,512]{1,0:T(8,128)}, f32[1024,512]{1,0:T(8,128)S(1)}, u32[]{:S(2)}, u32[]{:S(2)}) %collective-permute-start.1) | collective-permute-done | bytes 2097184 | tf_op jit(solution)/shard_map/ppermute | solution.py:14
  222.8 1.1 fusion.28
  223.9 0.7 copy-done.3
  224.6 2.1 multiply_convert_fusion
  226.8 1.0 fusion.24
  227.8 26.6 %all-gather.2.cloned.1.call-done = bf16[1024,512]{1,0:T(8,128)(2,1)} async-done(((bf16[256,512]{1,0:T(8,128)(2,1)}), bf16[1024,512]{1,0:T(8,128)(2,1)}) %all-gather.2.cloned.1.call-update) | async-done | bytes 1048592 | tf_op jit(solution)/shard_map/all_gather | solution.py:90
  254.5 2.5 broadcast_in_dim.46
  257.0 62.3 %while.21 = (s32[]{:T(128)}, f32[32,64,512]{2,1,0:T(8,128)}, s32[4,32]{1,0:T(4,128)S(1)}, bf16[4,32,64,64]{2,3,1,0:T(8,128)(2,1)}, s32[4,32]{1,0:T(4,128)S(1)}, /*index=5*/bf16[16,64,512]{2,1,0:T(8,128)(2,1)}, s32[]{:T(128)}) while((s32[]{:T(128)}, f32[32,64,512]{2,1,0:T(8,128)}, s32[4,32]{1,0:T(4,128)S(1)}, ...), condition=%wide.region_5.6_spmd, body=%wide.region_3.5_spmd.sunk | while | flops 136316288 | bytes 23598240 | solution.py:99
  257.0 1.9 gather_fusion.1
  258.9 3.7 fusion.61
  262.7 9.7 %scatter_fusion.1 = f32[32,64,512]{2,1,0:T(8,128)} fusion(f32[32,64,512]{2,1,0:T(8,128)} %get-tuple-element.225, s32[32]{0:T(128)S(1)} %get-tuple-element.194, f32[32,64,512]{2,1,0:T(8,128)} %fusion.61), kind=kCustom, calls=%fused_computation.4.clone.1 | custom fusion | flops 1048576 | bytes 12583040 | tf_op jit(solution)/shard_map/while/body/eval_jaxpr/scatter-add | solution.py:97
  272.4 1.9 gather_fusion.1
  274.4 3.7 fusion.61
  278.1 9.9 %scatter_fusion.1 = f32[32,64,512]{2,1,0:T(8,128)} fusion(f32[32,64,512]{2,1,0:T(8,128)} %get-tuple-element.225, s32[32]{0:T(128)S(1)} %get-tuple-element.194, f32[32,64,512]{2,1,0:T(8,128)} %fusion.61), kind=kCustom, calls=%fused_computation.4.clone.1 | custom fusion | flops 1048576 | bytes 12583040 | tf_op jit(solution)/shard_map/while/body/eval_jaxpr/scatter-add | solution.py:97
  288.0 1.9 gather_fusion.1
  289.9 3.8 fusion.61
  293.7 9.9 %scatter_fusion.1 = f32[32,64,512]{2,1,0:T(8,128)} fusion(f32[32,64,512]{2,1,0:T(8,128)} %get-tuple-element.225, s32[32]{0:T(128)S(1)} %get-tuple-element.194, f32[32,64,512]{2,1,0:T(8,128)} %fusion.61), kind=kCustom, calls=%fused_computation.4.clone.1 | custom fusion | flops 1048576 | bytes 12583040 | tf_op jit(solution)/shard_map/while/body/eval_jaxpr/scatter-add | solution.py:97
  303.6 1.9 gather_fusion.1
  305.6 3.7 fusion.61
  309.3 10.0 %scatter_fusion.1 = f32[32,64,512]{2,1,0:T(8,128)} fusion(f32[32,64,512]{2,1,0:T(8,128)} %get-tuple-element.225, s32[32]{0:T(128)S(1)} %get-tuple-element.194, f32[32,64,512]{2,1,0:T(8,128)} %fusion.61), kind=kCustom, calls=%fused_computation.4.clone.1 | custom fusion | flops 1048576 | bytes 12583040 | tf_op jit(solution)/shard_map/while/body/eval_jaxpr/scatter-add | solution.py:97
  319.3 2.8 slice.22
  322.1 15.8 %all-to-all-start.1 = ((bf16[128,8,512]{2,1,0:T(8,128)(2,1)}), bf16[128,8,512]{2,1,0:T(8,128)(2,1)}, u32[]{:S(2)}, u32[]{:S(2)}) async-start(bf16[128,8,512]{2,1,0:T(8,128)(2,1)} %bitcast.21), calls=%async_computation.1 | async-start | bytes 2097152 | tf_op jit(solution)/shard_map/all_to_all | solution.py:109
  338.0 1.9 slice.11
  339.9 28.2 %all-to-all-done.1 = bf16[128,8,512]{2,1,0:T(8,128)(2,1)} async-done(((bf16[128,8,512]{2,1,0:T(8,128)(2,1)}), bf16[128,8,512]{2,1,0:T(8,128)(2,1)}, u32[]{:S(2)}, u32[]{:S(2)}) %all-to-all-start.1) | async-done | bytes 1048608 | tf_op jit(solution)/shard_map/all_to_all | solution.py:109
  368.0 8.0 %scatter_custom_fusion.2 = f32[1024,512]{1,0:T(8,128)S(1)} fusion(f32[1024,512]{1,0:T(8,128)S(1)} %bitcast.86, s32[1024]{0:T(1024)S(1)} %bitcast.89, bf16[128,8,512]{2,1,0:T(8,128)(2,1)} %all-to-all-done.1), kind=kCustom, calls=%fused_computation.45 | custom fusion | flops 1048576 | bytes 3145728 | tf_op jit(solution)/shard_map/scatter-add | solution.py:113
  376.0 1.1 convert_element_type.58
  377.1 1.3 fusion.29
  378.4 1.3 fusion.35
  379.7 104.5 %all-reduce.2 = (bf16[512,512]{1,0:T(8,128)(2,1)}, bf16[512,512]{1,0:T(8,128)(2,1)}) all-reduce(f32[512,512]{1,0:T(8,128)S(1)} %fusion.29, f32[512,512]{1,0:T(8,128)S(1)} %fusion.35), channel_id=1, replica_groups=mesh['wide'=128,'rep'=4] {'wide','rep'}, use_global_device_ids=true, to_apply=%region_8.9 | all-reduce | flops 524288 | bytes 3145728 | tf_op jit(solution)/shard_map/psum | solution.py:88
  484.2 2.0 fusion.25
  (54 shorter events, 1.0 us)
Async XLA Ops:
  7.2 217.5 %copy-start = (bf16[512,512]{1,0:T(8,128)(2,1)S(1)}, bf16[512,512]{1,0:T(8,128)(2,1)}, u32[]{:S(2)}) copy-start(bf16[512,512]{1,0:T(8,128)(2,1)} %param.15) | copy-start | bytes 1572868
  14.3 20.2 %copy-start.6 = (s32[1,1,128]{2,1,0:T(1,128)S(1)}, s32[1,1,128]{2,1,0:T(1,128)}, u32[]{:S(2)}) copy-start(s32[1,1,128]{2,1,0:T(1,128)} %param.17) | copy-start | bytes 1540
  14.3 20.9 %copy-start.4 = (s32[1,1,32768]{2,1,0:T(1,128)S(1)}, s32[1,1,32768]{2,1,0:T(1,128)}, u32[]{:S(2)}) copy-start(s32[1,1,32768]{2,1,0:T(1,128)} %param.19) | copy-start | bytes 393220
  15.5 48.9 %all-to-all-start = ((bf16[128,8,512]{2,1,0:T(8,128)(2,1)}), bf16[128,8,512]{2,1,0:T(8,128)(2,1)S(1)}, u32[]{:S(2)}, u32[]{:S(2)}) async-start(bf16[128,8,512]{2,1,0:T(8,128)(2,1)} %bitcast_select_fusion), calls=%async_computation | async-start | bytes 2097152 | tf_op jit(solution)/shard_map/all_to_all | solution.py:48
  34.0 220.5 %all-gather.2.cloned.1.call-start = ((), (), s32[]{:S(2)}) async-start(), calls=%async_computation.3 | async-start | bytes 1310720 | tf_op jit(solution)/shard_map/all_gather | solution.py:90
  41.9 3.1 copy-start.7
  46.1 18.3 %copy-start.1 = (bf16[1024,512]{1,0:T(8,128)(2,1)S(1)}, bf16[1024,512]{1,0:T(8,128)(2,1)}, u32[]{:S(2)}) copy-start(bf16[1024,512]{1,0:T(8,128)(2,1)} %param.13) | copy-start | bytes 3145732
  124.7 54.4 %copy-start.5 = (s32[1024]{0:T(1024)S(1)}, s32[1024]{0:T(1024)}, u32[]{:S(2)}) copy-start(s32[1024]{0:T(1024)} %param.20) | copy-start | bytes 12292
  124.7 54.5 %copy-start.2 = (bf16[512,512]{1,0:T(8,128)(2,1)S(1)}, bf16[512,512]{1,0:T(8,128)(2,1)}, u32[]{:S(2)}) copy-start(bf16[512,512]{1,0:T(8,128)(2,1)} %param.14) | copy-start | bytes 1572868
  124.7 47.8 %collective-permute-start = (f32[1024,512]{1,0:T(8,128)S(1)}, f32[1024,512]{1,0:T(8,128)S(1)}, u32[]{:S(2)}, u32[]{:S(2)}) collective-permute-start(f32[1024,512]{1,0:T(8,128)S(1)} %bitcast.82), channel_id=1, source_target_pairs={{0,1},{1,0},{2,3},{3,2},{4,5},{5,4},{6,7},{7,6},{8,9},{9,8},{10,11... | collective-permute-start | bytes 6291464 | tf_op jit(solution)/shard_map/ppermute | solution.py:14
  174.3 48.4 %collective-permute-start.1 = (f32[1024,512]{1,0:T(8,128)}, f32[1024,512]{1,0:T(8,128)S(1)}, u32[]{:S(2)}, u32[]{:S(2)}) collective-permute-start(f32[1024,512]{1,0:T(8,128)} %bitcast_add_fusion), channel_id=1, source_target_pairs={{0,2},{1,3},{2,0},{3,1},{4,6},{5,7},{6,4},{7,5},{8,10},{9,11},{10,... | collective-permute-start | bytes 6291464 | tf_op jit(solution)/shard_map/ppermute | solution.py:14
  223.9 0.7 copy-start.3
  322.1 45.9 %all-to-all-start.1 = ((bf16[128,8,512]{2,1,0:T(8,128)(2,1)}), bf16[128,8,512]{2,1,0:T(8,128)(2,1)}, u32[]{:S(2)}, u32[]{:S(2)}) async-start(bf16[128,8,512]{2,1,0:T(8,128)(2,1)} %bitcast.21), calls=%async_computation.1 | async-start | bytes 2097152 | tf_op jit(solution)/shard_map/all_to_all | solution.py:109
  337.9 146.3 %reduce-scatter.2.cloned.1.call-start = ((), (), s32[]{:S(2)}) async-start(), calls=%async_computation.4 | async-start | bytes 1310720 | tf_op jit(solution)/shard_map/reduce_scatter | solution.py:115
Sparse Core Ops, SparseCore 0:
  228.0 26.4 all-gather.1
  377.3 20.4 reduce-scatter.1
